TPU v7x, 32 devices: a whole 2x2x4 slice. The times are simulated.
32 devices in a mesh: freq: 4 (over y, x), clus: 8 (over z, core).
Axes of the slice: x: 2, y: 2, z: 4, core: 2. Of those that a mesh axis runs over, the one named last changes fastest.
Arguments:
- history: bfloat16 [1024, 8, 1024], P('freq', None, 'clus'), may hold values from -6 to 6
- near_blocks: bfloat16 [8, 4, 512, 2, 128, 128], P('clus', None, 'freq'), may hold values from -0.1875 to 0.1875
- near_list: int32 [8, 4], replicated, may hold values from 0 to 7, as said below
- basis_out: bfloat16 [512, 2, 32, 1024], P('freq', None, None, 'clus'), may hold values from -0.75 to 0.75
- basis_in: bfloat16 [512, 2, 32, 1024], P('freq', None, None, 'clus'), may hold values from -0.375 to 0.375
- coupling: bfloat16 [8, 512, 2, 32, 256], P('clus', 'freq'), may hold values from -0.375 to 0.375
- ranks: int32 [8, 512, 8], P('clus', 'freq'), may hold values from 4 to 32
Outputs:
- potential: bfloat16 [512, 2, 8, 1024], P('freq', None, None, 'clus')
Inputs may be any that keep to these rules, and one draw needn't show every extreme that they name: `near_list`: row t starts with t itself; its other 3 entries are distinct shards other than t, each (t + d) mod 8 for some d with 1 <= |d| <= 3.
All inputs are finite; a program needn't handle non-finite values.
Results may differ from a plain program's by a relative error of at most 0.0055.
Values may be sent and summed in bfloat16 or wider, within the bound.
A program may use at most 128 MiB of HBM per device.

v0:
```python
import functools
import math

import jax
import jax.numpy as jnp
from jax import lax
from jax.experimental import pallas as pl
from jax.experimental.pallas import tpu as pltpu
from jax.sharding import PartitionSpec as P

LANES = 128
NT = (((1,), (1,)), ((), ()))
NN = (((1,), (0,)), ((), ()))


def dot(left, right, dims):
    return lax.dot_general(left, right, dims, preferred_element_type=jnp.float32)


def wave_factors(first_wave, count, total):
    waves = (first_wave + lax.iota(jnp.int32, count))[:, None]

    def factor(steps, scale):
        angle = (waves * steps[None, :] % total).astype(jnp.float32) * (2.0 * math.pi / total)
        weight = jnp.exp(steps.astype(jnp.float32) * (-math.log(2.0) / total)) * scale
        return weight[None, :] * jnp.cos(angle), -weight[None, :] * jnp.sin(angle)

    coarse = factor(lax.iota(jnp.int32, total // LANES) * LANES, 1.0)
    fine = factor(lax.iota(jnp.int32, LANES), total ** (-0.5))
    return coarse + fine


CHUNKS = 4
MESH = pl.DeviceIdType.MESH


def fill_tables(coarse_re, coarse_im, fine_re, fine_im, table):
    waves = fine_re.shape[0]
    chunk = waves // CHUNKS
    for a in range(coarse_re.shape[1]):
        c_re, c_im = coarse_re[:, a : a + 1], coarse_im[:, a : a + 1]
        f_re, f_im = fine_re[...], fine_im[...]
        for part, value in ((0, c_re * f_re - c_im * f_im), (1, c_re * f_im + c_im * f_re)):
            high = value.astype(jnp.bfloat16)
            low = (value - high.astype(jnp.float32)).astype(jnp.bfloat16)
            for w in range(CHUNKS):
                for piece, held in ((0, high), (1, low)):
                    rows = pl.ds((2 * piece + part) * chunk, chunk)
                    table[w, rows, a * LANES : (a + 1) * LANES] = held[w * chunk : (w + 1) * chunk]


def join(by_re, by_im, quarter):
    real = [r[:quarter] - m[quarter:] for r, m in zip(by_re, by_im)]
    imag = [r[quarter:] + m[:quarter] for r, m in zip(by_re, by_im)]
    return jnp.concatenate(real, 0), jnp.concatenate(imag, 0)


def transform_chunk(w, h, hist, table, sums, buf, me):
    blocks, exc, length = hist.shape[0], hist.shape[1], hist.shape[2]
    half = table.shape[1] // 2
    chunk = half // 2
    quarter = exc // 2
    for e in range(0, quarter, 2):
        value = None
        for f in range(blocks):
            steps = jnp.concatenate([hist[f, h * quarter + e], hist[f, h * quarter + e + 1]], axis=1)
            term = dot(table[w, :, f * length : (f + 1) * length], steps, NN)
            value = term if value is None else value + term
        value = value[:half] + value[half:]
        for part in range(2):
            for side in range(2):
                sums[pl.ds(part * quarter + e + side, chunk, stride=exc), :] = value[
                    part * chunk : (part + 1) * chunk, side * LANES : (side + 1) * LANES
                ]
    buf[me] = sums[...].reshape(chunk, exc, LANES).astype(jnp.bfloat16)


def compress_chunk(w, pair, coeffs, basis_in, me):
    chunk, exc, rank = pair[0].shape[1], pair[0].shape[2], basis_in.shape[2]
    pack = LANES // rank
    lane = lax.broadcasted_iota(jnp.int32, (exc, LANES), 1) // rank

    def step(group, carry):
        left = jnp.concatenate(
            [buf[me, pl.ds(group * pack, pack)].reshape(pack * exc, LANES) for buf in pair], axis=0
        )

        def pick(part):
            right = basis_in[pl.ds(w * chunk + group * pack, pack), part]
            full = dot(left, right.reshape(pack * rank, LANES), NT)
            outs = []
            for h in range(2):
                rows = full[h * pack * exc : (h + 1) * pack * exc]
                out = rows[:exc]
                for i in range(1, pack):
                    out = jnp.where(lane == i, rows[i * exc : (i + 1) * exc], out)
                outs.append(out)
            return outs

        real, imag = join(pick(0), pick(1), exc // 2)
        coeffs[me, w * (chunk // pack) + group] = jnp.concatenate([real, imag], 0).astype(jnp.bfloat16)
        return carry

    lax.fori_loop(0, chunk // pack, step, 0)


def far_groups(first, count, coeffs, couple, basis_out, limit, far):
    rank = couple.shape[2]
    sources, rows = coeffs.shape[0], coeffs.shape[2]
    half = rows // 2
    pack = LANES // rank
    unroll = min(2, count)
    position = lax.broadcasted_iota(jnp.int32, (rank, sources * rank), 0)

    def step(pair, carry):
        groups = [first + pair * unroll + u for u in range(unroll)]
        waves = [(g * pack + i, i, u) for u, g in enumerate(groups) for i in range(pack)]
        packed = [[coeffs[s, g].astype(jnp.float32) for s in range(sources)] for g in groups]
        stacked = [
            jnp.concatenate([p[:, i * rank : (i + 1) * rank] for p in packed[u]], axis=1).astype(jnp.bfloat16)
            for _, i, u in waves
        ]
        mixes = []
        for (wave, _, _), left in zip(waves, stacked):
            keep = position < limit[pl.ds(wave, 1), :]
            parts = [couple[wave, part] for part in range(2)]
            mixes.append([dot(left, jnp.where(keep, v, jnp.zeros_like(v)), NT) for v in parts])
        mixed = [
            jnp.concatenate([r[:half] - m[half:], r[half:] + m[:half]], 0).astype(jnp.bfloat16)
            for r, m in mixes
        ]
        spread = [[dot(m, basis_out[wave, part], NN) for part in range(2)] for (wave, _, _), m in zip(waves, mixed)]
        for (wave, _, _), (r, m) in zip(waves, spread):
            far[wave, pl.ds(0, half)] = r[:half] - m[half:]
            far[wave, pl.ds(half, half)] = r[half:] + m[:half]
        return carry

    lax.fori_loop(0, count // unroll, step, 0)


def near_chunk(w, picked, near, pair, far, out):
    slots, chunk = near.shape[1], near.shape[2]
    panels = near.shape[4]
    exc = pair[0].shape[2]
    unroll = 4

    def step(group, carry):
        waves = [group * unroll + i for i in range(unroll)]
        sums = []
        for k in waves:
            left = jnp.concatenate(
                [jnp.concatenate([buf[s, k] for s in picked], axis=1) for buf in pair], axis=0
            )
            right = jnp.concatenate(
                [near[w, j, k].reshape(2 * panels, panels) for j in range(slots)], axis=1
            )
            sums.append(dot(left, right, NT))
        for k, both in zip(waves, sums):
            by_re = [both[:exc, :panels], both[exc:, :panels]]
            by_im = [both[:exc, panels:], both[exc:, panels:]]
            real, imag = join(by_re, by_im, exc // 2)
            wave = w * chunk + k
            out[wave, 0] = (real + far[wave, pl.ds(0, exc)]).astype(out.dtype)
            out[wave, 1] = (imag + far[wave, pl.ds(exc, exc)]).astype(out.dtype)
        return carry

    lax.fori_loop(0, chunk // unroll, step, 0)


def kernel(freqs, clusters, mine, c_re, c_im, f_re, f_im, limit, own, near_in, couple_in, out_in, in_in,
           out, hist, table, sums, near, couple, basis_out, basis_in, *rest):
    total = 2 * CHUNKS
    bufs = rest[: total + 1]
    coeffs = bufs[total]
    far, local_sem, near_sem, hist_send, hist_recv, send_sem, recv_sem = rest[total + 1 :]
    f, c = lax.axis_index("freq"), lax.axis_index("clus")
    z, core = c // 2, c % 2
    levels = clusters // 2
    has_up, has_down = z + 1 < levels, z > 0
    up, down, partner = c + 2, c - 2, c + 1 - 2 * core
    chunk = near.shape[2]
    square = freqs == 4
    beside, across = f + 1 - 2 * (f % 2), (f + 2) % freqs
    peers = [beside, across] if square else [(f + i) % freqs for i in range(1, freqs)]

    loads = [
        pltpu.make_async_copy(own, hist.at[f], local_sem.at[0]),
        pltpu.make_async_copy(in_in, basis_in, local_sem.at[1]),
        pltpu.make_async_copy(out_in, basis_out, local_sem.at[2]),
        pltpu.make_async_copy(couple_in.at[0], couple, local_sem.at[3]),
    ]
    blocks = [
        pltpu.make_async_copy(near_in.at[0, :, pl.ds(w * chunk, chunk)], near.at[w], near_sem.at[w])
        for w in range(CHUNKS)
    ]

    barrier = pltpu.get_barrier_semaphore()
    for peer in peers:
        pl.semaphore_signal(barrier, inc=1, device_id=(peer, c), device_id_type=MESH)
    pl.semaphore_signal(barrier, inc=1, device_id=(f, partner), device_id_type=MESH)

    @pl.when(has_up)
    def _():
        pl.semaphore_signal(barrier, inc=1, device_id=(f, up), device_id_type=MESH)

    @pl.when(has_down)
    def _():
        pl.semaphore_signal(barrier, inc=1, device_id=(f, down), device_id_type=MESH)

    loads[0].start()
    pl.semaphore_wait(barrier, len(peers) + 1 + jnp.where(z + 1 < levels, 1, 0) + jnp.where(z > 0, 1, 0))

    quarter = own.shape[0] // 4
    pieces = [pl.ds(q * quarter, quarter) for q in range(4)]

    def give(peer, slot, part, source, number):
        return pltpu.make_async_remote_copy(
            src_ref=source.at[pieces[part]], dst_ref=hist.at[slot, pieces[part]],
            send_sem=hist_send.at[number, part], recv_sem=hist_recv.at[slot, part],
            device_id=(peer, c), device_id_type=MESH,
        )

    def arrived(slot, part):
        give(peers[0], slot, part, hist.at[slot], 0).wait_recv()

    sent = []

    def send(*what):
        sent.append(give(*what))
        sent[-1].start()

    def give_half(h):
        for i in range(2):
            for number, peer in enumerate(peers):
                part = 2 * h + (i + number) % 2
                send(peer, f, part, own, number)

    def relay_half(h):
        if square:
            arrived(beside, 2 * h)
            send(across, beside, 2 * h, hist.at[beside], len(peers))
            arrived(across, 2 * h + 1)
            send(beside, across, 2 * h + 1, hist.at[across], len(peers))

    def finish_half(h):
        if square:
            corner = (beside + 2) % freqs
            order = [(beside, 1), (across, 0), (corner, 0), (corner, 1)]
        else:
            order = [(peer, part) for peer in peers for part in range(2)]
        for slot, part in order:
            arrived(slot, 2 * h + part)

    give_half(0)
    for copy in loads[1:] + blocks:
        copy.start()
    fill_tables(c_re, c_im, f_re, f_im, table)
    relay_half(0)
    give_half(1)
    finish_half(0)
    loads[0].wait()

    def pass_on(w, source, target, way):
        return pltpu.make_async_remote_copy(
            src_ref=bufs[w].at[source], dst_ref=bufs[w].at[source],
            send_sem=send_sem.at[w, source // 2, way], recv_sem=recv_sem.at[w, source],
            device_id=(f, target), device_id_type=MESH,
        )

    def when(flag, action):
        @pl.when(flag)
        def _():
            action()

    def send_own(w):
        when(has_up, lambda: pass_on(w, c, up, 0).start())
        when(has_down, lambda: pass_on(w, c, down, 1).start())
        pass_on(w, c, partner, 2).start()

    def relay(w, d):
        below, above = c - 2 * d, c + 2 * d

        def from_below():
            pass_on(w, below, partner, 2).wait_recv()
            when(has_up, lambda: pass_on(w, below, up, 0).start())
            pass_on(w, below, partner, 2).start()

        def from_above():
            pass_on(w, above, partner, 2).wait_recv()
            when(has_down, lambda: pass_on(w, above, down, 1).start())
            pass_on(w, above, partner, 2).start()

        when(z >= d, from_below)
        when(z + d < levels, from_above)

    def complete(w):
        pass_on(w, partner, partner, 2).wait_recv()
        for d in range(1, levels):
            below, above = partner - 2 * d, partner + 2 * d
            when(z >= d, lambda: pass_on(w, below, partner, 2).wait_recv())
            when(z + d < levels, lambda: pass_on(w, above, partner, 2).wait_recv())

    first, second = [2 * w for w in range(CHUNKS)], [2 * w + 1 for w in range(CHUNKS)]
    for w in range(CHUNKS):
        transform_chunk(w, 0, hist, table, sums, bufs[first[w]], c)
        send_own(first[w])
    relay_half(1)
    if levels > 1:
        for m in first:
            relay(m, 1)
    finish_half(1)
    for w in range(CHUNKS):
        transform_chunk(w, 1, hist, table, sums, bufs[second[w]], c)
        send_own(second[w])
    loads[1].wait()
    for w in range(CHUNKS):
        compress_chunk(w, (bufs[first[w]], bufs[second[w]]), coeffs, basis_in, c)
    send_own(total)
    for copy in loads[2:]:
        copy.wait()
    picked = [mine[j] for j in range(near.shape[1])]
    last = levels - 1
    for d in range(1, last):
        if d > 1:
            for m in first:
                relay(m, d)
            for m in [total] + second:
                relay(m, d)
        else:
            for m in second[:2] + [total] + second[2:]:
                relay(m, d)
    if last > 1:
        for m in first:
            relay(m, last)
    relay(total, last)
    complete(total)
    groups = coeffs.shape[1] // CHUNKS
    for w in range(CHUNKS):
        far_groups(w * groups, groups, coeffs, couple, basis_out, limit, far)
        relay(second[w], last)
    for w in range(CHUNKS):
        complete(first[w])
        complete(second[w])
        blocks[w].wait()
        near_chunk(w, picked, near, (bufs[first[w]], bufs[second[w]]), far, out)

    for copy in sent:
        copy.wait_send()
    for w in range(total + 1):
        when(has_up, lambda: pass_on(w, c, up, 0).wait_send())
        when(has_down, lambda: pass_on(w, c, down, 1).wait_send())
        pass_on(w, c, partner, 2).wait_send()
        for d in range(1, levels):
            below, above = c - 2 * d, c + 2 * d

            def below_sent():
                when(has_up, lambda: pass_on(w, below, up, 0).wait_send())
                pass_on(w, below, partner, 2).wait_send()

            def above_sent():
                when(has_down, lambda: pass_on(w, above, down, 1).wait_send())
                pass_on(w, above, partner, 2).wait_send()

            when(z >= d, below_sent)
            when(z + d < levels, above_sent)


def step_all(mine, factors, limit, turned, near_blocks, coupling, basis_out, basis_in, freqs, clusters):
    exc, length, panels = turned.shape
    waves, _, rank, _ = basis_in.shape
    slots = near_blocks.shape[1]
    chunk = waves // CHUNKS
    pack = LANES // rank
    rows = 2 * exc
    bf16 = jnp.bfloat16
    vmem, anywhere = pl.BlockSpec(memory_space=pltpu.VMEM), pl.BlockSpec(memory_space=pl.ANY)
    dma = pltpu.SemaphoreType.DMA
    return pl.pallas_call(
        functools.partial(kernel, freqs, clusters),
        out_shape=jax.ShapeDtypeStruct((waves, 2, exc, panels), bf16),
        in_specs=[pl.BlockSpec(memory_space=pltpu.SMEM)] + [vmem] * 6 + [anywhere] * 4,
        out_specs=vmem,
        scratch_shapes=[
            pltpu.VMEM((freqs, exc, length, panels), bf16),
            pltpu.VMEM((CHUNKS, 4 * chunk, freqs * length), bf16),
            pltpu.VMEM((chunk * exc, panels), jnp.float32),
            pltpu.VMEM((CHUNKS, slots, chunk, 2, panels, panels), bf16),
            pltpu.VMEM(coupling.shape[1:], bf16),
            pltpu.VMEM(basis_out.shape, bf16),
            pltpu.VMEM(basis_in.shape, bf16),
        ]
        + [pltpu.VMEM((clusters, chunk, exc, panels), bf16)] * (2 * CHUNKS)
        + [
            pltpu.VMEM((clusters, waves // pack, rows, LANES), bf16),
            pltpu.VMEM((waves, rows, panels), jnp.float32),
            dma((4,)),
            dma((CHUNKS,)),
            dma((freqs, 4)),
            dma((freqs, 4)),
            dma((2 * CHUNKS + 1, clusters // 2, 3)),
            dma((2 * CHUNKS + 1, clusters)),
        ],
        compiler_params=pltpu.CompilerParams(
            collective_id=0, has_side_effects=True, vmem_limit_bytes=60 * 1024 * 1024
        ),
    )(mine, *factors, limit, turned, near_blocks, coupling, basis_out, basis_in)


def local(history, near_blocks, near_list, basis_out, basis_in, coupling, ranks):
    steps_dev, exc, panels = history.shape
    waves_dev, _, rank, _ = basis_in.shape
    clusters = lax.axis_size("clus")
    freqs = lax.axis_size("freq")
    total = steps_dev * freqs
    mine = lax.dynamic_index_in_dim(near_list, lax.axis_index("clus"), 0, keepdims=False)
    nearby = jnp.any(mine[:, None] == lax.iota(jnp.int32, clusters)[None, :], axis=0)
    far = jnp.where(nearby[None, :], 0, ranks[0])
    within = lax.iota(jnp.int32, rank)
    limit = jnp.where(within[None, None, :] < far[:, :, None], far[:, :, None], 0)
    limit = limit.reshape(waves_dev, clusters * rank)
    factors = wave_factors(lax.axis_index("freq") * waves_dev, waves_dev, total)
    turned = jnp.transpose(history, (1, 0, 2))
    return step_all(
        mine, factors, limit, turned, near_blocks, coupling, basis_out, basis_in, freqs, clusters
    )


def solution(mesh):
    placed = (
        P("freq", None, "clus"),
        P("clus", None, "freq", None, None, None),
        P(),
        P("freq", None, None, "clus"),
        P("freq", None, None, "clus"),
        P("clus", "freq", None, None, None),
        P("clus", "freq", None),
    )
    return jax.shard_map(
        local, mesh=mesh, in_specs=placed, out_specs=P("freq", None, None, "clus"), check_vma=False
    )
```

profile of v0, /device:TPU:0, one launch (start us, length us, event | category | flops | bytes accessed | tf_op | source)
XLA Modules:
  0.0 86.2 jit_solution(2393973902948386552)
XLA Ops:
  0.0 0.0 copy-start
  0.0 0.7 copy-done
  0.7 0.2 dynamic-slice_reduce_fusion.mine
  0.9 0.0 copy-start.1
  0.9 0.1 fusion.9
  1.0 0.1 lt.40
  1.1 0.8 copy.21
  2.0 0.1 copy.23
  2.1 0.7 compare_select_fusion.limit
  2.7 1.0 %sine_multiply_fusion.1 = (f32[128,8]{1,0:T(8,128)}, f32[128,8]{1,0:T(8,128)}) fusion(f32[8]{0:T(128)S(1)} %get-tuple-element.10, s32[8]{0:T(128)S(1)} %iota_multiply_fusion, s32[128]{0:T(128)S(1)} %iota_add_fusion, f32[8]{0:T(128)S(1)} %get-tuple-element.9), kind=kLoop, calls=%fused_computation.21 | loop fusion | flops 16384 | bytes 8800 | tf_op jit(solution)/shard_map/mul | solution.py:26
  3.7 1.0 %sine_multiply_fusion = (f32[128,128]{1,0:T(8,128)}, f32[128,128]{1,0:T(8,128)}) fusion(f32[128]{0:T(128)S(1)} %get-tuple-element.12, s32[128]{0:T(128)S(1)} %iota_add_fusion, f32[128]{0:T(128)S(1)} %get-tuple-element.11), kind=kLoop, calls=%fused_computation.17 | loop fusion | flops 262144 | bytes 132608 | tf_op jit(solution)/shard_map/mul | solution.py:26
  4.7 1.9 %copy.28 = bf16[256,8,128]{2,0,1:T(8,128)(2,1)} copy(bf16[256,8,128]{2,1,0:T(8,128)(2,1)} %param.7) | data formatting | bytes 1048576 | tf_op args[0]
  6.6 0.0 copy-done.1
  6.6 77.7 %shard_map.73 = bf16[128,2,8,128]{3,2,1,0:T(8,128)(2,1)} custom-call(s32[4]{0:T(128)} %copy-done.1, f32[128,8]{1,0:T(8,128)} %get-tuple-element.6.c_re, f32[128,8]{1,0:T(8,128)} %get-tuple-element.5.c_im, f32[128,128]{1,0:T(8,128)} %get-tuple-element.8.f_re, f32[128,128]{1,0:T(8,128)} %get-tuple-element.7.f_im, s32[128,256]{1,0:T(8,128)} %compare_select_fusion.limit, ...), custom_call_target="tpu_custom_call" | custom-call | tf_op jit(solution)/shard_map/pallas_call | solution.py:378
  84.3 1.9 %copy.30 = bf16[128,2,8,128]{3,2,1,0:T(8,128)(2,1)} copy(bf16[128,2,8,128]{3,2,1,0:T(8,128)(2,1)} %shard_map.73) | data formatting | bytes 1048576
  (8 shorter events, 0.1 us)
Async XLA Ops:
  0.0 0.7 copy-start
  0.9 5.8 %copy-start.1 = (s32[4]{0:T(128)}, s32[4]{0:T(128)S(1)}, u32[]{:S(2)}) copy-start(s32[4]{0:T(128)S(1)} %dynamic-slice_reduce_fusion.mine) | copy-start | bytes 52
where the time goes:
time: 87.3 us; the launch traced here: 86.2 us
  Pallas kernels  77.7 us (89%)
  local copies, waits for them, and re-layouts  5.68 us (7%)
  other arithmetic  2.79 us (3%)
    pallas_call x1, Pallas kernels, step_all(): pl.pallas_call(functools.partial(kernel, freqs, clusters), out_shape=jax....  77.7 us
    unnamed x7, local copies, waits for them, and re-layouts  5.24 us
    mul x2, other arithmetic, factor(): return (weight[None, :] * jnp.cos(angle), -weight[None, :] * jnp.sin(angle))  2.01 us

commit v1 on v0

v1 whole, which is shorter than its diff:
```python
import functools
import math

import jax
import jax.numpy as jnp
import numpy as np
from jax import lax
from jax.experimental import pallas as pl
from jax.experimental.pallas import tpu as pltpu
from jax.sharding import PartitionSpec as P

LANES = 128
NT = (((1,), (1,)), ((), ()))
NN = (((1,), (0,)), ((), ()))
MESH = pl.DeviceIdType.MESH
GROUP = 4
CUTS = (2, 4, 6, 7, 8)
LOADS = 4
PERIOD = 16


def dot(left, right, dims):
    return lax.dot_general(left, right, dims, preferred_element_type=jnp.float32)


def wave_constants(freqs, waves, total):
    rows = np.arange(2 * freqs * waves)
    wave, part = GROUP * (rows // (2 * GROUP)) + rows % GROUP, (rows // GROUP) % 2

    def factor(steps, scale):
        angle = (wave[:, None] * steps[None, :] % total) * (2.0 * math.pi / total)
        weight = np.exp(steps * (-math.log(2.0) / total)) * scale
        return weight * np.cos(angle), -weight * np.sin(angle)

    f_re, f_im = factor(np.arange(LANES), total ** (-0.5))
    imag = (part == 1)[:, None]
    fine = np.stack([np.where(imag, f_im, f_re), np.where(imag, f_re, -f_im)])
    fine = fine.reshape(2, freqs, 2 * waves, LANES).transpose(1, 0, 2, 3)
    c_re, c_im = factor(np.arange(total // LANES) * LANES, 1.0)
    coarse = np.stack([c_re[:PERIOD], c_im[:PERIOD]]).transpose(2, 0, 1)
    coarse = np.broadcast_to(coarse[..., None], coarse.shape + (LANES,))
    return jnp.asarray(fine, jnp.float32), jnp.asarray(coarse, jnp.float32)


def fill_tables(coarse, fine, table):
    spans, rows, half = coarse.shape[0], fine.shape[1], table.shape[1] // 2
    repeat = rows // PERIOD

    def step(a, carry):
        p = fine[0].reshape(repeat, PERIOD, LANES)
        q = fine[1].reshape(repeat, PERIOD, LANES)
        value = (coarse[a, 0] * p + coarse[a, 1] * q).reshape(rows, LANES)
        high = value.astype(jnp.bfloat16)
        low = (value - high.astype(jnp.float32)).astype(jnp.bfloat16)
        lanes = pl.ds(pl.multiple_of(a * LANES, LANES), LANES)
        for p in range(2):
            table[p, :half, lanes] = high[p * half : (p + 1) * half]
            table[p, half:, lanes] = low[p * half : (p + 1) * half]
        return carry

    lax.fori_loop(0, spans, step, 0)


def transform(g, p, hist, table):
    blocks, length = hist.shape[0], hist.shape[2]
    half = table.shape[1] // 2
    value = None
    for f in range(blocks):
        steps = jnp.concatenate([hist[f, 2 * g], hist[f, 2 * g + 1]], axis=1)
        term = dot(table[p, :, f * length : (f + 1) * length], steps, NN)
        value = term if value is None else value + term
    value = value[:half] + value[half:]
    one, two = [value[:, i * LANES : (i + 1) * LANES].reshape(-1, 2 * GROUP, LANES) for i in range(2)]
    upper = lax.broadcasted_iota(jnp.int32, one.shape, 1) < GROUP
    real = jnp.where(upper, one, pltpu.roll(two, GROUP, 1))
    imag = jnp.where(upper, pltpu.roll(one, GROUP, 1), two)
    return jnp.concatenate([real, imag], axis=1).astype(jnp.bfloat16)


def pairs_of(both, width):
    rows = 2 * GROUP
    re, im = both[:, :width], both[:, width:]
    real, imag = [], []
    for g in range(both.shape[0] // (2 * rows)):
        a, b = 2 * g * rows, (2 * g + 1) * rows
        real.append(re[a : a + rows] - im[b : b + rows])
        imag.append(re[b : b + rows] + im[a : a + rows])
    return jnp.concatenate(real, 0), jnp.concatenate(imag, 0)


def kernel(freqs, clusters, near_list, ranks, fine_in, coarse_in, own, near_in, couple_in, out_in, in_in,
           out, raw, wide, hist, fine, coarse, table, near, couple, basis_out, basis_in, limit, far, spread, *rest):
    parts = len(CUTS)
    pre = [rest[0:2], rest[2:4]]
    post = rest[4 : 4 + parts]
    packs = rest[4 + parts : 6 + parts]
    local_sem, near_sem, hist_send, hist_recv, send_sem, recv_sem = rest[6 + parts :]
    f, c = lax.axis_index("freq"), lax.axis_index("clus")
    z, core = c // 2, c % 2
    levels = clusters // 2
    has_up, has_down = z + 1 < levels, z > 0
    up, down, partner = c + 2, c - 2, c + 1 - 2 * core
    square = freqs == 4
    beside, across = f + 1 - 2 * (f % 2), (f + 2) % freqs
    peers = [beside, across] if square else [(f + i) % freqs for i in range(1, freqs)]
    slots, waves, panels = near.shape[0], near.shape[1], near.shape[3]
    exc, rank, sources = hist.shape[1], basis_in.shape[2], clusters
    blocks = waves // GROUP
    half = blocks // 2
    ends = [blocks * cut // CUTS[-1] for cut in CUTS]
    starts = [0] + ends[:-1]

    loads = [
        pltpu.make_async_copy(own, raw, local_sem.at[0]),
        pltpu.make_async_copy(fine_in.at[f], fine, local_sem.at[1]),
        pltpu.make_async_copy(coarse_in, coarse, local_sem.at[2]),
        pltpu.make_async_copy(in_in, basis_in, local_sem.at[3]),
        pltpu.make_async_copy(couple_in.at[0], couple, local_sem.at[4]),
        pltpu.make_async_copy(out_in, basis_out, local_sem.at[5]),
    ]
    share = waves // LOADS
    chunks = [
        pltpu.make_async_copy(
            near_in.at[0, :, pl.ds(w * share, share)], near.at[:, pl.ds(w * share, share)], near_sem.at[w]
        )
        for w in range(LOADS)
    ]

    barrier = pltpu.get_barrier_semaphore()
    for peer in peers:
        pl.semaphore_signal(barrier, inc=1, device_id=(peer, c), device_id_type=MESH)
    pl.semaphore_signal(barrier, inc=1, device_id=(f, partner), device_id_type=MESH)

    def when(flag, action):
        @pl.when(flag)
        def _():
            action()

    when(has_up, lambda: pl.semaphore_signal(barrier, inc=1, device_id=(f, up), device_id_type=MESH))
    when(has_down, lambda: pl.semaphore_signal(barrier, inc=1, device_id=(f, down), device_id_type=MESH))
    for copy in loads[:3]:
        copy.start()

    sent = []

    def give(peer, slot, e, number):
        return pltpu.make_async_remote_copy(
            src_ref=hist.at[slot, e], dst_ref=hist.at[slot, e],
            send_sem=hist_send.at[number, e], recv_sem=hist_recv.at[slot, e],
            device_id=(peer, c), device_id_type=MESH,
        )

    def arrived(slot, e):
        give(peers[0], slot, e, 0).wait_recv()

    def send(*what):
        sent.append(give(*what))
        sent[-1].start()

    def turn(g):
        for e in (2 * g, 2 * g + 1):
            hist[f, e] = wide[:, e, :].astype(jnp.bfloat16)

    def give_pair(g):
        for i in range(2):
            for number, peer in enumerate(peers):
                send(peer, f, 2 * g + (i + number) % 2, number)

    def relay_pair(g):
        if square:
            arrived(beside, 2 * g)
            send(across, beside, 2 * g, len(peers))
            arrived(across, 2 * g + 1)
            send(beside, across, 2 * g + 1, len(peers))

    def finish_pair(g):
        if square:
            corner = (beside + 2) % freqs
            order = [(beside, 1), (across, 0), (corner, 0), (corner, 1)]
        else:
            order = [(peer, part) for peer in peers for part in range(2)]
        for slot, part in order:
            arrived(slot, 2 * g + part)

    units = [pre[0][0], pre[0][1], pre[1][0], pre[1][1], packs[0], packs[1]] + list(post)

    def pass_on(u, source, target, way):
        return pltpu.make_async_remote_copy(
            src_ref=units[u].at[source], dst_ref=units[u].at[source],
            send_sem=send_sem.at[u, source // 2, way], recv_sem=recv_sem.at[u, source],
            device_id=(f, target), device_id_type=MESH,
        )

    state = {"own": 0, "tick": 0}

    def send_own():
        u = state["own"]
        when(has_up, lambda: pass_on(u, c, up, 0).start())
        when(has_down, lambda: pass_on(u, c, down, 1).start())
        pass_on(u, c, partner, 2).start()
        state["own"] += 1

    def relay(u, d):
        below, above = c - 2 * d, c + 2 * d

        def from_below():
            pass_on(u, below, partner, 2).wait_recv()
            when(has_up, lambda: pass_on(u, below, up, 0).start())
            pass_on(u, below, partner, 2).start()

        def from_above():
            pass_on(u, above, partner, 2).wait_recv()
            when(has_down, lambda: pass_on(u, above, down, 1).start())
            pass_on(u, above, partner, 2).start()

        when(z >= d, from_below)
        when(z + d < levels, from_above)

    def pump(tick):
        while state["tick"] < tick:
            state["tick"] += 1
            for d in range(levels - 1, 0, -1):
                u = state["tick"] - d
                if 0 <= u < len(units):
                    relay(u, d)

    def complete(u):
        pump(u + levels - 1)
        pass_on(u, partner, partner, 2).wait_recv()
        for d in range(1, levels):
            below, above = partner - 2 * d, partner + 2 * d
            when(z >= d, lambda: pass_on(u, below, partner, 2).wait_recv())
            when(z + d < levels, lambda: pass_on(u, above, partner, 2).wait_recv())

    def make(g, p):
        value = transform(g, p, hist, table)
        if g < 2:
            pre[g][p][c] = value
            return
        for w in range(parts):
            if p * half <= starts[w] < (p + 1) * half:
                post[w][c, g - 2] = value[starts[w] - p * half : ends[w] - p * half]

    def compress(w):
        p = starts[w] // half
        lane = lax.broadcasted_iota(jnp.int32, (exc, LANES), 1) // rank

        def step(i, carry):
            b = starts[w] - p * half + i
            left = jnp.concatenate([pre[0][p][c, b], pre[1][p][c, b], post[w][c, 0, i], post[w][c, 1, i]], 0)
            first = (starts[w] + i) * GROUP
            right = [basis_in[pl.ds(first, GROUP), part].reshape(GROUP * rank, panels) for part in range(2)]
            pair = pairs_of(dot(left, jnp.concatenate(right, 0), NT), GROUP * rank)
            outs = []
            for part in range(2):
                spread[part] = pair[part]
                rows = spread[part, pl.ds(0, exc, stride=GROUP), :]
                for k in range(1, GROUP):
                    rows = jnp.where(lane == k, spread[part, pl.ds(k, exc, stride=GROUP), :], rows)
                outs.append(rows)
            packs[p][c, b] = jnp.concatenate(outs, 0).astype(jnp.bfloat16)
            return carry

        lax.fori_loop(0, ends[w] - starts[w], step, 0)

    def set_limits():
        width = sources * rank
        source = lax.broadcasted_iota(jnp.int32, (sources, width), 1) // rank
        keep = source == lax.broadcasted_iota(jnp.int32, (sources, width), 0)
        for j in range(slots):
            keep = keep & (source != near_list[j, c])
        turned = jnp.transpose(ranks[...].astype(jnp.float32)).astype(jnp.bfloat16)
        top = dot(turned, jnp.where(keep, 1.0, 0.0).astype(jnp.bfloat16), NN)
        within = (lax.broadcasted_iota(jnp.int32, top.shape, 1) % rank).astype(jnp.float32)
        limit[...] = jnp.where(within < top, top, 0.0)

    def far_half(p):
        unroll = min(2, half)
        rows = 2 * exc
        position = lax.broadcasted_iota(jnp.int32, (rank, sources * rank), 0).astype(jnp.float32)

        def step(pair, carry):
            local = [pair * unroll + u for u in range(unroll)]
            members = [((p * half + b) * GROUP + i, i, u) for u, b in enumerate(local) for i in range(GROUP)]
            packed = [[packs[p][s, b].astype(jnp.float32) for s in range(sources)] for b in local]
            stacked = [
                jnp.concatenate([v[:, i * rank : (i + 1) * rank] for v in packed[u]], axis=1).astype(jnp.bfloat16)
                for _, i, u in members
            ]
            mixes = []
            for (wave, _, _), left in zip(members, stacked):
                keep = position < limit[pl.ds(wave, 1), :]
                views = [couple[wave, part] for part in range(2)]
                mixes.append([dot(left, jnp.where(keep, v, jnp.zeros_like(v)), NT) for v in views])
            mixed = [
                jnp.concatenate([r[:exc] - m[exc:], r[exc:] + m[:exc]], 0).astype(jnp.bfloat16) for r, m in mixes
            ]
            sums = [[dot(m, basis_out[wave, part], NN) for part in range(2)] for (wave, _, _), m in zip(members, mixed)]
            for (wave, _, _), (r, m) in zip(members, sums):
                far[wave, pl.ds(0, exc)] = r[:exc] - m[exc:]
                far[wave, pl.ds(exc, rows - exc)] = r[exc:] + m[:exc]
            return carry

        lax.fori_loop(0, half // unroll, step, 0)

    picked = [near_list[j, c] for j in range(slots)]

    def near_part(w):
        p = starts[w] // half
        mine = lax.broadcasted_iota(jnp.int32, (GROUP * exc, panels), 0) % GROUP

        def step(i, carry):
            b = starts[w] - p * half + i
            views = [[pre[0][p][s, b], pre[1][p][s, b], post[w][s, 0, i], post[w][s, 1, i]] for s in picked]
            left = jnp.concatenate([jnp.concatenate(v, 0) for v in views], 1)
            first = (starts[w] + i) * GROUP
            total = None
            for k in range(GROUP):
                right = [near[j, first + k].reshape(2 * panels, panels) for j in range(slots)]
                pair = pairs_of(dot(left, jnp.concatenate(right, 1), NT), panels)
                total = pair if total is None else [jnp.where(mine == k, v, t) for v, t in zip(pair, total)]
            for part in range(2):
                spread[part] = total[part]
            for k in range(GROUP):
                for part in range(2):
                    rows = spread[part, pl.ds(k, exc, stride=GROUP), :]
                    out[first + k, part] = (rows + far[first + k, pl.ds(part * exc, exc)]).astype(out.dtype)
            return carry

        lax.fori_loop(0, ends[w] - starts[w], step, 0)

    loads[0].wait()
    wide[...] = raw[...].astype(jnp.float32)
    turn(0)
    pl.semaphore_wait(barrier, len(peers) + 1 + jnp.where(z + 1 < levels, 1, 0) + jnp.where(z > 0, 1, 0))
    give_pair(0)
    for copy in loads[3:] + chunks:
        copy.start()
    for g in range(1, exc // 2):
        turn(g)
    for copy in loads[1:3]:
        copy.wait()
    fill_tables(coarse, fine, table)
    set_limits()

    last = exc // 2 - 1
    for g in range(exc // 2):
        relay_pair(g)
        if g < last:
            give_pair(g + 1)
        pump(min(2 * g - 1, 2 * len(pre)))
        finish_pair(g)
        for p in range(2):
            make(g, p)
            if g < 2:
                send_own()
    loads[3].wait()
    for w in range(parts):
        compress(w)
        if ends[w] % half == 0:
            send_own()
    pump(len(pre) * 2 + 1)
    send_own()
    pump(len(pre) * 2 + 2)
    send_own()
    for copy in loads[4:]:
        copy.wait()
    for p in range(2):
        complete(4 + p)
        far_half(p)
        send_own()
    while state["own"] < len(units):
        send_own()
    ready = 0
    for w in range(parts):
        if starts[w] % half == 0:
            for g in range(2):
                complete(2 * g + starts[w] // half)
        complete(6 + w)
        while ready < LOADS and ready * share < ends[w] * GROUP:
            chunks[ready].wait()
            ready += 1
        near_part(w)

    for copy in sent:
        copy.wait_send()
    for u in range(len(units)):
        when(has_up, lambda: pass_on(u, c, up, 0).wait_send())
        when(has_down, lambda: pass_on(u, c, down, 1).wait_send())
        pass_on(u, c, partner, 2).wait_send()
        for d in range(1, levels):
            below, above = c - 2 * d, c + 2 * d

            def below_sent():
                when(has_up, lambda: pass_on(u, below, up, 0).wait_send())
                pass_on(u, below, partner, 2).wait_send()

            def above_sent():
                when(has_down, lambda: pass_on(u, above, down, 1).wait_send())
                pass_on(u, above, partner, 2).wait_send()

            when(z >= d, below_sent)
            when(z + d < levels, above_sent)


def local(history, near_blocks, near_list, basis_out, basis_in, coupling, ranks):
    length, exc, panels = history.shape
    waves, _, rank, _ = basis_in.shape
    clusters = lax.axis_size("clus")
    freqs = lax.axis_size("freq")
    slots = near_blocks.shape[1]
    total = length * freqs
    blocks = waves // GROUP
    half = blocks // 2
    rows = 2 * exc
    bf16, f32 = jnp.bfloat16, jnp.float32
    fine, coarse = wave_constants(freqs, waves, total)
    ends = [blocks * cut // CUTS[-1] for cut in CUTS]
    sizes = [b - a for a, b in zip([0] + ends[:-1], ends)]
    vmem, anywhere = pl.BlockSpec(memory_space=pltpu.VMEM), pl.BlockSpec(memory_space=pl.ANY)
    dma = pltpu.SemaphoreType.DMA
    units = 6 + len(CUTS)
    return pl.pallas_call(
        functools.partial(kernel, freqs, clusters),
        out_shape=jax.ShapeDtypeStruct((waves, 2, exc, panels), bf16),
        in_specs=[pl.BlockSpec(memory_space=pltpu.SMEM), vmem] + [anywhere] * 7,
        out_specs=vmem,
        scratch_shapes=[
            pltpu.VMEM(history.shape, bf16),
            pltpu.VMEM(history.shape, f32),
            pltpu.VMEM((freqs, exc, length, panels), bf16),
            pltpu.VMEM(fine.shape[1:], f32),
            pltpu.VMEM(coarse.shape, f32),
            pltpu.VMEM((2, 2 * waves, total), bf16),
            pltpu.VMEM(near_blocks.shape[1:], bf16),
            pltpu.VMEM(coupling.shape[1:], bf16),
            pltpu.VMEM(basis_out.shape, bf16),
            pltpu.VMEM(basis_in.shape, bf16),
            pltpu.VMEM((waves, clusters * rank), f32),
            pltpu.VMEM((waves, rows, panels), f32),
            pltpu.VMEM((2, GROUP * exc, panels), f32),
        ]
        + [pltpu.VMEM((clusters, half, 4 * GROUP, panels), bf16)] * 4
        + [pltpu.VMEM((clusters, 2, size, 4 * GROUP, panels), bf16) for size in sizes]
        + [pltpu.VMEM((clusters, half, rows, GROUP * rank), bf16)] * 2
        + [
            dma((6,)),
            dma((LOADS,)),
            dma((freqs, exc)),
            dma((freqs, exc)),
            dma((units, clusters // 2, 3)),
            dma((units, clusters)),
        ],
        compiler_params=pltpu.CompilerParams(
            collective_id=0, has_side_effects=True, vmem_limit_bytes=60 * 1024 * 1024
        ),
    )(near_list.T, ranks[0].T, fine, coarse, history, near_blocks, coupling, basis_out, basis_in)


def solution(mesh):
    placed = (
        P("freq", None, "clus"),
        P("clus", None, "freq", None, None, None),
        P(),
        P("freq", None, None, "clus"),
        P("freq", None, None, "clus"),
        P("clus", "freq", None, None, None),
        P("clus", "freq", None),
    )
    return jax.shard_map(
        local, mesh=mesh, in_specs=placed, out_specs=P("freq", None, None, "clus"), check_vma=False
    )
```

time: 87.3 us -> 76.6 us (0.88); the launches traced: 86.2 us -> 76.4 us
  local copies, waits for them, and re-layouts: 5.68 us -> 1.87 us
  Pallas kernels: 77.7 us -> 74.5 us
  other arithmetic: 2.79 us -> 0 us
    unnamed x7 -> x1, local copies, waits for them, and re-layouts: 5.24 us -> 1.87 us
    pallas_call x1, Pallas kernels: 77.7 us -> 74.5 us  [local(): pl.pallas_call(functools.partial(kernel, freqs, clusters), out_shape=jax....]
    mul x4 -> x0, other arithmetic: 2.02 us -> none  [the longest x2 2.01 us: factor(): return (weight[None, :] * jnp.cos(angle), -weight[None, :] * jnp.sin(angle))]
where the time goes in v1:
time: 76.6 us; the launch traced here: 76.4 us
  Pallas kernels  74.5 us (97%)
  local copies, waits for them, and re-layouts  1.87 us (2%)
    pallas_call x1, Pallas kernels, local(): pl.pallas_call(functools.partial(kernel, freqs, clusters), out_shape=jax....  74.5 us
    unnamed x1, local copies, waits for them, and re-layouts  1.87 us

profile of v1, /device:TPU:0, one launch (start us, length us, event | category | flops | bytes accessed | tf_op | source)
XLA Modules:
  0.0 76.4 jit_solution(17966393988656680350)
XLA Ops:
  0.0 74.5 %shard_map.91 = bf16[128,2,8,128]{3,2,1,0:T(8,128)(2,1)} custom-call(s32[4,8]{1,0:T(4,128)} %bitcast.5, s32[8,128]{1,0:T(8,128)} %bitcast.4, f32[4,2,256,128]{3,2,1,0:T(8,128)} %constant.4.clone.fine_in, f32[8,2,16,128]{3,2,1,0:T(8,128)} %constant.5.clone.coarse_in, bf16[256,8,128]{2,1,0:T(8,128)(2,1)} %own.1, bf16[1,4,128,2,128,128]{5,4,3,2,1,0:T(8,128)(2,1)} %near_in.1, ...), custom_call_target="tpu_custom_call" | custom-call | tf_op jit(solution)/shard_map/pallas_call | solution.py:423
  74.5 1.9 %copy.11 = bf16[128,2,8,128]{3,2,1,0:T(8,128)(2,1)} copy(bf16[128,2,8,128]{3,2,1,0:T(8,128)(2,1)} %shard_map.91) | data formatting | bytes 1048576

commit v2 on v1

--- a/solution.py
+++ b/solution.py
@@ -17,6 +17,8 @@
 CUTS = (2, 4, 6, 7, 8)
 LOADS = 4
 PERIOD = 16
+UNROLL = 4
+KEEP = 5
 
 
 def dot(left, right, dims):
@@ -89,12 +91,11 @@
 
 
 def kernel(freqs, clusters, near_list, ranks, fine_in, coarse_in, own, near_in, couple_in, out_in, in_in,
-           out, raw, wide, hist, fine, coarse, table, near, couple, basis_out, basis_in, limit, far, spread, *rest):
+           result, out, raw, wide, hist, fine, coarse, table, near, couple, basis_out, basis_in, limit, far, spread, *rest):
     parts = len(CUTS)
     pre = [rest[0:2], rest[2:4]]
     post = rest[4 : 4 + parts]
-    packs = rest[4 + parts : 6 + parts]
-    local_sem, near_sem, hist_send, hist_recv, send_sem, recv_sem = rest[6 + parts :]
+    local_sem, near_sem, out_sem, hist_send, hist_recv, send_sem, recv_sem = rest[4 + parts :]
     f, c = lax.axis_index("freq"), lax.axis_index("clus")
     z, core = c // 2, c % 2
     levels = clusters // 2
@@ -159,12 +160,11 @@
 
     def turn(g):
         for e in (2 * g, 2 * g + 1):
-            hist[f, e] = wide[:, e, :].astype(jnp.bfloat16)
-
-    def give_pair(g):
-        for i in range(2):
-            for number, peer in enumerate(peers):
-                send(peer, f, 2 * g + (i + number) % 2, number)
+            hist[f, e] = wide[pl.ds(e, hist.shape[2], stride=exc), :].astype(jnp.bfloat16)
+
+    def give_part(g, i):
+        for number, peer in enumerate(peers):
+            send(peer, f, 2 * g + (i + number) % 2, number)
 
     def relay_pair(g):
         if square:
@@ -182,19 +182,20 @@
         for slot, part in order:
             arrived(slot, 2 * g + part)
 
-    units = [pre[0][0], pre[0][1], pre[1][0], pre[1][1], packs[0], packs[1]] + list(post)
+    units = [pre[0][0], pre[0][1], pre[1][0], pre[1][1]] + list(post)
 
     def pass_on(u, source, target, way):
         return pltpu.make_async_remote_copy(
             src_ref=units[u].at[source], dst_ref=units[u].at[source],
-            send_sem=send_sem.at[u, source // 2, way], recv_sem=recv_sem.at[u, source],
+            send_sem=send_sem.at[u % KEEP, source // 2, way], recv_sem=recv_sem.at[u, source],
             device_id=(f, target), device_id_type=MESH,
         )
 
-    state = {"own": 0, "tick": 0}
+    state = {"own": 0}
 
     def send_own():
         u = state["own"]
+        drain(u - KEEP)
         when(has_up, lambda: pass_on(u, c, up, 0).start())
         when(has_down, lambda: pass_on(u, c, down, 1).start())
         pass_on(u, c, partner, 2).start()
@@ -216,16 +217,23 @@
         when(z >= d, from_below)
         when(z + d < levels, from_above)
 
+    passed = set()
+
+    def pass_unit(u, *hops):
+        for d in hops:
+            if d < levels and (u, d) not in passed:
+                assert u < state["own"]
+                passed.add((u, d))
+                relay(u, d)
+
     def pump(tick):
-        while state["tick"] < tick:
-            state["tick"] += 1
+        for t in range(1, tick + 1):
             for d in range(levels - 1, 0, -1):
-                u = state["tick"] - d
-                if 0 <= u < len(units):
-                    relay(u, d)
+                if 0 <= t - d < len(units):
+                    pass_unit(t - d, d)
 
     def complete(u):
-        pump(u + levels - 1)
+        pass_unit(u, *range(1, levels))
         pass_on(u, partner, partner, 2).wait_recv()
         for d in range(1, levels):
             below, above = partner - 2 * d, partner + 2 * d
@@ -245,23 +253,32 @@
         p = starts[w] // half
         lane = lax.broadcasted_iota(jnp.int32, (exc, LANES), 1) // rank
 
-        def step(i, carry):
-            b = starts[w] - p * half + i
-            left = jnp.concatenate([pre[0][p][c, b], pre[1][p][c, b], post[w][c, 0, i], post[w][c, 1, i]], 0)
-            first = (starts[w] + i) * GROUP
-            right = [basis_in[pl.ds(first, GROUP), part].reshape(GROUP * rank, panels) for part in range(2)]
-            pair = pairs_of(dot(left, jnp.concatenate(right, 0), NT), GROUP * rank)
-            outs = []
-            for part in range(2):
-                spread[part] = pair[part]
-                rows = spread[part, pl.ds(0, exc, stride=GROUP), :]
-                for k in range(1, GROUP):
-                    rows = jnp.where(lane == k, spread[part, pl.ds(k, exc, stride=GROUP), :], rows)
-                outs.append(rows)
-            packs[p][c, b] = jnp.concatenate(outs, 0).astype(jnp.bfloat16)
+        count = ends[w] - starts[w]
+        unroll = math.gcd(count, UNROLL)
+
+        def step(turn, carry):
+            pairs = []
+            for n in range(unroll):
+                i = turn * unroll + n
+                b = starts[w] - p * half + i
+                left = jnp.concatenate([pre[0][p][c, b], pre[1][p][c, b], post[w][c, 0, i], post[w][c, 1, i]], 0)
+                first = (starts[w] + i) * GROUP
+                right = [basis_in[pl.ds(first, GROUP), part].reshape(GROUP * rank, panels) for part in range(2)]
+                pairs.append(pairs_of(dot(left, jnp.concatenate(right, 0), NT), GROUP * rank))
+            for n, pair in enumerate(pairs):
+                for part in range(2):
+                    spread[n, part] = pair[part]
+            for n in range(unroll):
+                outs = []
+                for part in range(2):
+                    rows = spread[n, part, pl.ds(0, exc, stride=GROUP), :]
+                    for k in range(1, GROUP):
+                        rows = jnp.where(lane == k, spread[n, part, pl.ds(k, exc, stride=GROUP), :], rows)
+                    outs.append(rows)
+                post[w][c, 2, turn * unroll + n] = jnp.concatenate(outs, 0).astype(jnp.bfloat16)
             return carry
 
-        lax.fori_loop(0, ends[w] - starts[w], step, 0)
+        lax.fori_loop(0, count // unroll, step, 0)
 
     def set_limits():
         width = sources * rank
@@ -274,15 +291,16 @@
         within = (lax.broadcasted_iota(jnp.int32, top.shape, 1) % rank).astype(jnp.float32)
         limit[...] = jnp.where(within < top, top, 0.0)
 
-    def far_half(p):
-        unroll = min(2, half)
+    def far_part(w):
+        count = ends[w] - starts[w]
+        unroll = math.gcd(count, 2)
         rows = 2 * exc
         position = lax.broadcasted_iota(jnp.int32, (rank, sources * rank), 0).astype(jnp.float32)
 
         def step(pair, carry):
             local = [pair * unroll + u for u in range(unroll)]
-            members = [((p * half + b) * GROUP + i, i, u) for u, b in enumerate(local) for i in range(GROUP)]
-            packed = [[packs[p][s, b].astype(jnp.float32) for s in range(sources)] for b in local]
+            members = [((starts[w] + b) * GROUP + i, i, u) for u, b in enumerate(local) for i in range(GROUP)]
+            packed = [[post[w][s, 2, b].astype(jnp.float32) for s in range(sources)] for b in local]
             stacked = [
                 jnp.concatenate([v[:, i * rank : (i + 1) * rank] for v in packed[u]], axis=1).astype(jnp.bfloat16)
                 for _, i, u in members
@@ -301,7 +319,7 @@
                 far[wave, pl.ds(exc, rows - exc)] = r[exc:] + m[:exc]
             return carry
 
-        lax.fori_loop(0, half // unroll, step, 0)
+        lax.fori_loop(0, count // unroll, step, 0)
 
     picked = [near_list[j, c] for j in range(slots)]
 
@@ -309,98 +327,154 @@
         p = starts[w] // half
         mine = lax.broadcasted_iota(jnp.int32, (GROUP * exc, panels), 0) % GROUP
 
-        def step(i, carry):
-            b = starts[w] - p * half + i
-            views = [[pre[0][p][s, b], pre[1][p][s, b], post[w][s, 0, i], post[w][s, 1, i]] for s in picked]
-            left = jnp.concatenate([jnp.concatenate(v, 0) for v in views], 1)
-            first = (starts[w] + i) * GROUP
-            total = None
-            for k in range(GROUP):
-                right = [near[j, first + k].reshape(2 * panels, panels) for j in range(slots)]
-                pair = pairs_of(dot(left, jnp.concatenate(right, 1), NT), panels)
-                total = pair if total is None else [jnp.where(mine == k, v, t) for v, t in zip(pair, total)]
-            for part in range(2):
-                spread[part] = total[part]
-            for k in range(GROUP):
+        count = ends[w] - starts[w]
+        unroll = math.gcd(count, 2)
+
+        def step(turn, carry):
+            totals = []
+            for n in range(unroll):
+                i = turn * unroll + n
+                b = starts[w] - p * half + i
+                views = [[pre[0][p][s, b], pre[1][p][s, b], post[w][s, 0, i], post[w][s, 1, i]] for s in picked]
+                left = jnp.concatenate([jnp.concatenate(v, 0) for v in views], 1)
+                first = (starts[w] + i) * GROUP
+                total = None
+                for k in range(GROUP):
+                    right = [near[j, first + k].reshape(2 * panels, panels) for j in range(slots)]
+                    pair = pairs_of(dot(left, jnp.concatenate(right, 1), NT), panels)
+                    total = pair if total is None else [jnp.where(mine == k, v, t) for v, t in zip(pair, total)]
+                totals.append(total)
+            for n, total in enumerate(totals):
+                first = (starts[w] + turn * unroll + n) * GROUP
                 for part in range(2):
-                    rows = spread[part, pl.ds(k, exc, stride=GROUP), :]
-                    out[first + k, part] = (rows + far[first + k, pl.ds(part * exc, exc)]).astype(out.dtype)
+                    spread[n, part] = total[part]
+                for k in range(GROUP):
+                    for part in range(2):
+                        rows = spread[n, part, pl.ds(k, exc, stride=GROUP), :]
+                        out[first + k, part] = (rows + far[first + k, pl.ds(part * exc, exc)]).astype(out.dtype)
             return carry
 
-        lax.fori_loop(0, ends[w] - starts[w], step, 0)
+        lax.fori_loop(0, count // unroll, step, 0)
+
+    def deliver(w):
+        span = pl.ds(starts[w] * GROUP, (ends[w] - starts[w]) * GROUP)
+        return pltpu.make_async_copy(out.at[span], result.at[span], out_sem.at[w])
+
+    drained = set()
+
+    def drain(u):
+        if u < 0 or u in drained:
+            return
+        drained.add(u)
+        pass_unit(u, *range(1, levels))
+        when(has_up, lambda: pass_on(u, c, up, 0).wait_send())
+        when(has_down, lambda: pass_on(u, c, down, 1).wait_send())
+        pass_on(u, c, partner, 2).wait_send()
+        for d in range(1, levels):
+            below, above = c - 2 * d, c + 2 * d
+
+            def below_sent():
+                when(has_up, lambda: pass_on(u, below, up, 0).wait_send())
+                pass_on(u, below, partner, 2).wait_send()
+
+            def above_sent():
+                when(has_down, lambda: pass_on(u, above, down, 1).wait_send())
+                pass_on(u, above, partner, 2).wait_send()
+
+            when(z >= d, below_sent)
+            when(z + d < levels, above_sent)
 
     loads[0].wait()
-    wide[...] = raw[...].astype(jnp.float32)
+    wide[...] = raw[...].astype(jnp.float32).reshape(wide.shape)
     turn(0)
     pl.semaphore_wait(barrier, len(peers) + 1 + jnp.where(z + 1 < levels, 1, 0) + jnp.where(z > 0, 1, 0))
-    give_pair(0)
-    for copy in loads[3:] + chunks:
-        copy.start()
+    give_part(0, 0)
     for g in range(1, exc // 2):
         turn(g)
     for copy in loads[1:3]:
         copy.wait()
     fill_tables(coarse, fine, table)
     set_limits()
-
-    last = exc // 2 - 1
-    for g in range(exc // 2):
-        relay_pair(g)
-        if g < last:
-            give_pair(g + 1)
-        pump(min(2 * g - 1, 2 * len(pre)))
-        finish_pair(g)
+    give_part(0, 1)
+    for copy in loads[3:] + chunks:
+        copy.start()
+
+    def give_pair(g):
+        give_part(g, 0)
+        give_part(g, 1)
+
+    def make_pair(g):
         for p in range(2):
             make(g, p)
             if g < 2:
                 send_own()
+
+    relay_pair(0)
+    give_pair(1)
+    finish_pair(0)
+    make_pair(0)
+    relay_pair(1)
+    give_pair(2)
+    finish_pair(1)
+    make_pair(1)
+    relay_pair(2)
+    give_pair(3)
+    pass_unit(0, 1)
+    pass_unit(1, 1)
+    finish_pair(2)
+    make_pair(2)
+    relay_pair(3)
+    pass_unit(0, 2)
+    pass_unit(2, 1)
+    pass_unit(1, 2)
+    pass_unit(3, 1)
+    finish_pair(3)
+    make_pair(3)
     loads[3].wait()
-    for w in range(parts):
+    compress(0)
+    send_own()
+    pass_unit(2, 2)
+    pass_unit(3, 2)
+    compress(1)
+    pass_unit(0, 3)
+    pass_unit(1, 3)
+    pass_unit(4, 1)
+    send_own()
+    compress(2)
+    for copy in sent:
+        copy.wait_send()
+    pass_unit(4, 2)
+    pass_unit(5, 1)
+    send_own()
+    pass_unit(2, 3)
+    pass_unit(3, 3)
+    for w in range(3, parts):
         compress(w)
-        if ends[w] % half == 0:
-            send_own()
-    pump(len(pre) * 2 + 1)
-    send_own()
-    pump(len(pre) * 2 + 2)
-    send_own()
     for copy in loads[4:]:
         copy.wait()
-    for p in range(2):
-        complete(4 + p)
-        far_half(p)
-        send_own()
-    while state["own"] < len(units):
-        send_own()
     ready = 0
     for w in range(parts):
+        pump(6 + w)
+        if state["own"] < len(units):
+            send_own()
+        complete(4 + w)
+        far_part(w)
+        pump(7 + w)
+        if 5 + w < len(units):
+            pass_unit(5 + w, *range(1, levels))
+        drain(w)
+        while ready < LOADS and ready * share < ends[w] * GROUP:
+            chunks[ready].wait()
+            ready += 1
         if starts[w] % half == 0:
             for g in range(2):
                 complete(2 * g + starts[w] // half)
-        complete(6 + w)
-        while ready < LOADS and ready * share < ends[w] * GROUP:
-            chunks[ready].wait()
-            ready += 1
         near_part(w)
-
-    for copy in sent:
-        copy.wait_send()
+        deliver(w).start()
     for u in range(len(units)):
-        when(has_up, lambda: pass_on(u, c, up, 0).wait_send())
-        when(has_down, lambda: pass_on(u, c, down, 1).wait_send())
-        pass_on(u, c, partner, 2).wait_send()
-        for d in range(1, levels):
-            below, above = c - 2 * d, c + 2 * d
-
-            def below_sent():
-                when(has_up, lambda: pass_on(u, below, up, 0).wait_send())
-                pass_on(u, below, partner, 2).wait_send()
-
-            def above_sent():
-                when(has_down, lambda: pass_on(u, above, down, 1).wait_send())
-                pass_on(u, above, partner, 2).wait_send()
-
-            when(z >= d, below_sent)
-            when(z + d < levels, above_sent)
+        drain(u)
+    for w in range(parts):
+        deliver(w).wait()
 
 
 def local(history, near_blocks, near_list, basis_out, basis_in, coupling, ranks):
@@ -419,15 +493,16 @@
     sizes = [b - a for a, b in zip([0] + ends[:-1], ends)]
     vmem, anywhere = pl.BlockSpec(memory_space=pltpu.VMEM), pl.BlockSpec(memory_space=pl.ANY)
     dma = pltpu.SemaphoreType.DMA
-    units = 6 + len(CUTS)
+    units = 4 + len(CUTS)
     return pl.pallas_call(
         functools.partial(kernel, freqs, clusters),
         out_shape=jax.ShapeDtypeStruct((waves, 2, exc, panels), bf16),
         in_specs=[pl.BlockSpec(memory_space=pltpu.SMEM), vmem] + [anywhere] * 7,
-        out_specs=vmem,
+        out_specs=anywhere,
         scratch_shapes=[
+            pltpu.VMEM((waves, 2, exc, panels), bf16),
             pltpu.VMEM(history.shape, bf16),
-            pltpu.VMEM(history.shape, f32),
+            pltpu.VMEM((length * exc, panels), f32),
             pltpu.VMEM((freqs, exc, length, panels), bf16),
             pltpu.VMEM(fine.shape[1:], f32),
             pltpu.VMEM(coarse.shape, f32),
@@ -438,17 +513,17 @@
             pltpu.VMEM(basis_in.shape, bf16),
             pltpu.VMEM((waves, clusters * rank), f32),
             pltpu.VMEM((waves, rows, panels), f32),
-            pltpu.VMEM((2, GROUP * exc, panels), f32),
+            pltpu.VMEM((UNROLL, 2, GROUP * exc, panels), f32),
         ]
         + [pltpu.VMEM((clusters, half, 4 * GROUP, panels), bf16)] * 4
-        + [pltpu.VMEM((clusters, 2, size, 4 * GROUP, panels), bf16) for size in sizes]
-        + [pltpu.VMEM((clusters, half, rows, GROUP * rank), bf16)] * 2
+        + [pltpu.VMEM((clusters, 3, size, 4 * GROUP, panels), bf16) for size in sizes]
         + [
             dma((6,)),
             dma((LOADS,)),
+            dma((len(CUTS),)),
+            dma((3 if freqs == 4 else freqs, exc)),
             dma((freqs, exc)),
-            dma((freqs, exc)),
-            dma((units, clusters // 2, 3)),
+            dma((KEEP, clusters // 2, 3)),
             dma((units, clusters)),
         ],
         compiler_params=pltpu.CompilerParams(

time: 76.6 us -> 70.7 us (0.923)
  Pallas kernels: 74.5 us -> 68.6 us
    pallas_call x1, Pallas kernels: 74.5 us -> 68.6 us  [local(): pl.pallas_call(functools.partial(kernel, freqs, clusters), out_shape=jax....]
where the time goes in v2:
time: 70.7 us; the launch traced here: 70.5 us
  Pallas kernels  68.6 us (97%)
  local copies, waits for them, and re-layouts  1.87 us (3%)
    pallas_call x1, Pallas kernels, local(): pl.pallas_call(functools.partial(kernel, freqs, clusters), out_shape=jax....  68.6 us
    unnamed x1, local copies, waits for them, and re-layouts  1.87 us

profile of v2, /device:TPU:0, one launch (start us, length us, event | category | flops | bytes accessed | tf_op | source)
XLA Modules:
  0.0 70.5 jit_solution(16016415868861861934)
XLA Ops:
  0.0 68.6 %shard_map.91 = bf16[128,2,8,128]{3,2,1,0:T(8,128)(2,1)} custom-call(s32[4,8]{1,0:T(4,128)} %bitcast.5, s32[8,128]{1,0:T(8,128)} %bitcast.4, f32[4,2,256,128]{3,2,1,0:T(8,128)} %constant.4.clone.fine_in, f32[8,2,16,128]{3,2,1,0:T(8,128)} %constant.5.clone.coarse_in, bf16[256,8,128]{2,1,0:T(8,128)(2,1)} %own.1, bf16[1,4,128,2,128,128]{5,4,3,2,1,0:T(8,128)(2,1)} %near_in.1, ...), custom_call_target="tpu_custom_call" | custom-call | tf_op jit(solution)/shard_map/pallas_call | solution.py:497
  68.6 1.9 %copy.11 = bf16[128,2,8,128]{3,2,1,0:T(8,128)(2,1)} copy(bf16[128,2,8,128]{3,2,1,0:T(8,128)(2,1)} %shard_map.91) | data formatting | bytes 1048576
